TPU v7x, 32 devices: a whole 2x2x4 slice. The times are simulated.
32 devices in a mesh: seq: 8 (over z, y), head: 4 (over x, core).
Axes of the slice: x: 2, y: 2, z: 4, core: 2. Of those that a mesh axis runs over, the one named last changes fastest.
Arguments:
- tokens: bfloat16 [1024, 1024], P('seq'), may hold values from -6 to 6
- cotangent: bfloat16 [1024, 1024], P('seq'), may hold values from -6 to 6
- gate_code: int32 [2, 1024, 8], P(None, 'seq', 'head'), may hold values from 0 to 723000
- beta_code: int32 [2, 1024, 8], P(None, 'seq', 'head'), may hold values from 256 to 1024
- norm1_gain: float32 [2, 1024], replicated, may hold values from 0.5 to 1.5
- weight_in: bfloat16 [2, 1024, 6144], P(None, None, 'head'), may hold values from -0.1875 to 0.1875
- conv_weight: bfloat16 [2, 4, 4096], P(None, None, 'head'), may hold values from -3 to 3
- out_gain: float32 [2, 256], replicated, may hold values from 0.5 to 1.5
- weight_out: bfloat16 [2, 2048, 1024], P(None, 'head'), may hold values from -0.25 to 0.25
- norm2_gain: float32 [2, 1024], replicated, may hold values from 0.5 to 1.5
- weight_gate: bfloat16 [2, 1024, 2816], P(None, None, 'head'), may hold values from -0.1875 to 0.1875
- weight_up: bfloat16 [2, 1024, 2816], P(None, None, 'head'), may hold values from -0.1875 to 0.1875
- weight_down: bfloat16 [2, 2816, 1024], P(None, 'head'), may hold values from -0.21875 to 0.21875
Outputs:
- activations: bfloat16 [1024, 1024], P('seq')
- input_grad: float32 [1024, 1024], P('seq')
- grad_norm1_gain: float32 [2, 1024], replicated
- grad_weight_in: float32 [2, 1024, 6144], P(None, 'seq', 'head')
- grad_conv_weight: float32 [2, 4, 4096], P(None, None, 'head')
- grad_out_gain: float32 [2, 256], replicated
- grad_weight_out: float32 [2, 2048, 1024], P(None, 'head', 'seq')
- grad_norm2_gain: float32 [2, 1024], replicated
- grad_weight_gate: float32 [2, 1024, 2816], P(None, 'seq', 'head')
- grad_weight_up: float32 [2, 1024, 2816], P(None, 'seq', 'head')
- grad_weight_down: float32 [2, 2816, 1024], P(None, 'head', 'seq')
All inputs are finite; a program needn't handle non-finite values.
Results may differ from a plain program's by a relative error of at most 0.02.
Values sent between devices are 32-bit elements; how exact they have to be, the bound alone decides.
No kernel may reach another device: no remote copies, remote signals or barrier semaphores. Data moves between devices by JAX's collectives and lax.ppermute only.
A program may use at most 256 MiB of HBM per device.

v0:
```python
import jax
import jax.numpy as jnp
from jax import lax
from jax.sharding import PartitionSpec as P

DK = 128
DV = 256
CONV = 4
SPAN = 64
STACK_LEVELS = 2
highest = lax.Precision.HIGHEST
norm_eps = 1e-06
gate_unit = 1.0 / 1048576.0
beta_unit = 1.0 / 1024.0


def from_behind(array, axis, by):
    length = lax.axis_size(axis)
    pairs = [(i, i + by) for i in range(length) if 0 <= i + by < length]
    return lax.ppermute(array, axis, pairs)


def rms_norm(stream, gain):
    return stream * lax.rsqrt(jnp.mean(stream * stream, axis=-1, keepdims=True) + norm_eps) * gain


def unit_rows(vectors):
    return vectors * lax.rsqrt(jnp.sum(vectors * vectors, axis=-1, keepdims=True) + norm_eps)


def swiglu(gate_pre, up_pre):
    return jax.nn.silu(gate_pre) * up_pre


def post_mix(outputs, gate_z, gain):
    return rms_norm(outputs, gain) * jax.nn.silu(gate_z)


def mixer_inputs(windowed, conv_taps):
    length_total = windowed.shape[0] - (CONV - 1)
    conv_out = conv_taps[0] * windowed[CONV - 1 :]
    for tap_index in range(1, CONV):
        conv_out = (
            conv_out
            + conv_taps[tap_index]
            * windowed[CONV - 1 - tap_index : CONV - 1 - tap_index + length_total]
        )
    active = jax.nn.silu(conv_out).reshape(length_total, -1, 2 * DK + DV)
    queries = unit_rows(active[:, :, :DK]) * DK ** (-0.5)
    keys_unit = unit_rows(active[:, :, DK : 2 * DK])
    return (queries, keys_unit, active[:, :, 2 * DK :])


def span_step(carry_state, pieces):
    queries, keys_unit, values_in, logdecay, beta_rate = pieces
    block_len = queries.shape[0]
    cumulated = jnp.cumsum(logdecay, axis=0)
    cum_heads = jnp.transpose(cumulated)
    row_index = lax.broadcasted_iota(jnp.int32, (1, block_len, block_len), 1)
    col_index = lax.broadcasted_iota(jnp.int32, (1, block_len, block_len), 2)
    inclusive = row_index >= col_index
    log_ratio = jnp.where(inclusive, cum_heads[:, :, None] - cum_heads[:, None, :], 0.0)
    decay_ratio = jnp.where(inclusive, jnp.exp(log_ratio), 0.0)
    beta_heads = jnp.transpose(beta_rate)
    key_key = jnp.einsum("thd,shd->hts", keys_unit, keys_unit, precision=highest)
    strict_lower = jnp.where(
        row_index > col_index, beta_heads[:, :, None] * decay_ratio * key_key, 0.0
    )
    system = strict_lower + jnp.eye(block_len, dtype=strict_lower.dtype)[None]
    decay_all = jnp.exp(cumulated)
    right_side = jnp.concatenate(
        [beta_rate[:, :, None] * values_in, (beta_rate * decay_all)[:, :, None] * keys_unit], axis=2
    )
    right_side = jnp.transpose(right_side, (1, 0, 2))
    solved_system = lax.linalg.triangular_solve(system, right_side, left_side=True, lower=True)
    val_width = values_in.shape[2]
    new_values = solved_system[:, :, :val_width] - jnp.einsum(
        "htd,hvd->htv", solved_system[:, :, val_width:], carry_state, precision=highest
    )
    query_key = jnp.einsum("thd,shd->hts", queries, keys_unit, precision=highest)
    mixing = decay_ratio * query_key
    outputs = jnp.transpose(decay_all)[:, :, None] * jnp.einsum(
        "thd,hvd->htv", queries, carry_state, precision=highest
    )
    outputs = outputs + jnp.einsum("hts,hsv->htv", mixing, new_values, precision=highest)
    to_end = jnp.exp(cumulated[-1][None, :] - cumulated)
    new_state = jnp.exp(cumulated[-1])[:, None, None] * carry_state
    new_state = new_state + jnp.einsum(
        "hsv,shd->hvd", new_values, to_end[:, :, None] * keys_unit, precision=highest
    )
    return (new_state, jnp.transpose(outputs, (1, 0, 2)))


def delta_rule(queries, keys_unit, values_in, logdecay, beta_rate, carry_state):
    length_total = queries.shape[0]
    block_count = length_total // SPAN

    def blocks(tensor):
        return tensor.reshape((block_count, SPAN) + tensor.shape[1:])

    final_state, outputs = lax.scan(
        span_step,
        carry_state,
        (
            blocks(queries),
            blocks(keys_unit),
            blocks(values_in),
            blocks(logdecay),
            blocks(beta_rate),
        ),
    )
    return (outputs.reshape((length_total,) + outputs.shape[2:]), final_state)


def state_prefix(transfer, offset):
    all_transfer, all_offset = (
        lax.all_gather(transfer, "seq", axis=0, tiled=True),
        lax.all_gather(offset, "seq", axis=0, tiled=True),
    )
    devices = lax.axis_size("seq")
    position = lax.axis_index("seq")
    transfer_kept = all_transfer.reshape((devices,) + transfer.shape)
    offsets_all = all_offset.reshape((devices,) + offset.shape)

    def advance(index_now, carry_state):
        moved = (
            jnp.einsum("hvj,hjk->hvk", carry_state, transfer_kept[index_now], precision=highest)
            + offsets_all[index_now]
        )
        return jnp.where(index_now < position, moved, carry_state)

    incoming = lax.fori_loop(0, devices, advance, jnp.zeros_like(offset))
    return (incoming, transfer_kept)


def state_back(transfer_kept, local_grad):
    all_grad = lax.all_gather(local_grad, "seq", axis=0, tiled=True)
    devices = lax.axis_size("seq")
    position = lax.axis_index("seq")
    grads_all = all_grad.reshape((devices,) + local_grad.shape)

    def retreat(step_index, carry_state):
        index_now = devices - 1 - step_index
        moved = (
            jnp.einsum("hvj,hkj->hvk", carry_state, transfer_kept[index_now], precision=highest)
            + grads_all[index_now]
        )
        return jnp.where(index_now > position, moved, carry_state)

    outgoing = lax.fori_loop(0, devices, retreat, jnp.zeros_like(local_grad))
    return outgoing


def head_total(partial_sum):
    share = lax.psum_scatter(partial_sum, "head", scatter_dimension=1, tiled=True)
    return lax.all_gather(share, "head", axis=1, tiled=True)


def layer_forward(stream, logdecay, beta_rate, weights):
    (
        gain_one,
        weight_in,
        conv_weight,
        out_gain,
        weight_out,
        gain_two,
        weight_gate,
        weight_up,
        weight_down,
    ) = weights
    length_total = stream.shape[0]
    normed = rms_norm(stream, gain_one).astype(jnp.bfloat16)
    projected = jnp.dot(normed, weight_in, preferred_element_type=jnp.float32).reshape(
        length_total, -1, 2 * DK + 2 * DV
    )
    head_count = projected.shape[1]
    conv_input = projected[:, :, : 2 * DK + DV].reshape(length_total, -1)
    gate_z = projected[:, :, 2 * DK + DV :]
    before = from_behind(conv_input[length_total - (CONV - 1) :], "seq", 1)
    windowed = jnp.concatenate([before, conv_input], axis=0)
    conv_taps = conv_weight.astype(jnp.float32)
    queries, keys_unit, values_in = mixer_inputs(windowed, conv_taps)
    wide_values = jnp.concatenate(
        [values_in, jnp.zeros((length_total, head_count, DK), jnp.float32)], axis=2
    )
    start_state = jnp.concatenate(
        [
            jnp.zeros((head_count, DV, DK), jnp.float32),
            jnp.broadcast_to(jnp.eye(DK, dtype=jnp.float32), (head_count, DK, DK)),
        ],
        axis=1,
    )
    wide_out, wide_end = delta_rule(
        queries, keys_unit, wide_values, logdecay, beta_rate, start_state
    )
    carried = wide_out[:, :, DV:]
    incoming, transfer_kept = state_prefix(wide_end[:, DV:], wide_end[:, :DV])
    outputs = wide_out[:, :, :DV] + jnp.einsum("thd,hvd->thv", carried, incoming, precision=highest)
    gated_out = post_mix(outputs, gate_z, out_gain).reshape(length_total, -1).astype(jnp.bfloat16)
    stream_mid = stream + head_total(
        jnp.dot(gated_out, weight_out, preferred_element_type=jnp.float32)
    )
    second_normed = rms_norm(stream_mid, gain_two).astype(jnp.bfloat16)
    gate_pre = jnp.dot(second_normed, weight_gate, preferred_element_type=jnp.float32)
    up_pre = jnp.dot(second_normed, weight_up, preferred_element_type=jnp.float32)
    hidden = swiglu(gate_pre, up_pre).astype(jnp.bfloat16)
    stream_next = stream_mid + head_total(
        jnp.dot(hidden, weight_down, preferred_element_type=jnp.float32)
    )
    stored = (
        stream,
        normed,
        windowed,
        conv_taps,
        gate_z,
        queries,
        keys_unit,
        values_in,
        outputs,
        carried,
        incoming,
        transfer_kept,
        gated_out,
        stream_mid,
        second_normed,
        gate_pre,
        up_pre,
        hidden,
    )
    return (stream_next, stored)


def layer_backward(grad_stream, logdecay, beta_rate, weights, stored):
    (
        gain_one,
        weight_in,
        conv_weight,
        out_gain,
        weight_out,
        gain_two,
        weight_gate,
        weight_up,
        weight_down,
    ) = weights
    (
        stream,
        normed,
        windowed,
        conv_taps,
        gate_z,
        queries,
        keys_unit,
        values_in,
        outputs,
        carried,
        incoming,
        transfer_kept,
        gated_out,
        stream_mid,
        second_normed,
        gate_pre,
        up_pre,
        hidden,
    ) = stored
    length_total = grad_stream.shape[0]
    back_bf = grad_stream.astype(jnp.bfloat16)
    grad_down = jnp.dot(hidden.T, back_bf, preferred_element_type=jnp.float32)
    grad_hidden = jnp.dot(back_bf, weight_down.T, preferred_element_type=jnp.float32)
    _, act_pull = jax.vjp(swiglu, gate_pre, up_pre)
    grad_gate_pre, grad_up_pre = act_pull(grad_hidden)
    grad_gate_pre = grad_gate_pre.astype(jnp.bfloat16)
    grad_up_pre = grad_up_pre.astype(jnp.bfloat16)
    grad_gate = jnp.dot(second_normed.T, grad_gate_pre, preferred_element_type=jnp.float32)
    grad_up = jnp.dot(second_normed.T, grad_up_pre, preferred_element_type=jnp.float32)
    ffn_partial = jnp.dot(
        grad_gate_pre, weight_gate.T, preferred_element_type=jnp.float32
    ) + jnp.dot(grad_up_pre, weight_up.T, preferred_element_type=jnp.float32)
    grad_normed_two = lax.psum(ffn_partial, "head")
    _, norm_pull = jax.vjp(rms_norm, stream_mid, gain_two)
    grad_mid, grad_gain_two = norm_pull(grad_normed_two)
    grad_stream = grad_stream + grad_mid
    back_bf = grad_stream.astype(jnp.bfloat16)
    grad_out = jnp.dot(gated_out.T, back_bf, preferred_element_type=jnp.float32)
    grad_gated = jnp.dot(back_bf, weight_out.T, preferred_element_type=jnp.float32).reshape(
        length_total, -1, DV
    )
    _, post_pull = jax.vjp(post_mix, outputs, gate_z, out_gain)
    grad_outputs, grad_gate_z, gain_mid_part = post_pull(grad_gated)
    local_grad = jnp.einsum("thv,thd->hvd", grad_outputs, carried, precision=highest)
    outgoing = state_back(transfer_kept, local_grad)

    def core_rule(queries, keys_unit, values_in):
        return delta_rule(queries, keys_unit, values_in, logdecay, beta_rate, incoming)

    _, rule_pull = jax.vjp(core_rule, queries, keys_unit, values_in)
    grad_queries, grad_keys, grad_values = rule_pull((grad_outputs, outgoing))
    _, mix_pull = jax.vjp(mixer_inputs, windowed, conv_taps)
    grad_window, grad_conv = mix_pull((grad_queries, grad_keys, grad_values))
    from_next = from_behind(grad_window[: CONV - 1], "seq", -1)
    grad_conv_in = grad_window[CONV - 1 :] + jnp.pad(
        from_next, ((length_total - (CONV - 1), 0), (0, 0))
    )
    grad_proj = (
        jnp.concatenate([grad_conv_in.reshape(length_total, -1, 2 * DK + DV), grad_gate_z], axis=2)
        .reshape(length_total, -1)
        .astype(jnp.bfloat16)
    )
    grad_in = jnp.dot(normed.T, grad_proj, preferred_element_type=jnp.float32)
    mixer_partial = jnp.dot(grad_proj, weight_in.T, preferred_element_type=jnp.float32)
    grad_normed, grad_out_gain = lax.psum((mixer_partial, gain_mid_part), "head")
    _, norm_pull = jax.vjp(rms_norm, stream, gain_one)
    grad_prev, grad_gain_one = norm_pull(grad_normed)
    return (
        grad_stream + grad_prev,
        (
            grad_gain_one,
            grad_in,
            grad_conv,
            grad_out_gain,
            grad_out,
            grad_gain_two,
            grad_gate,
            grad_up,
            grad_down,
        ),
    )


def body(
    tokens,
    cotangent,
    gate_code,
    beta_code,
    norm1_gain,
    weight_in,
    conv_weight,
    out_gain,
    weight_out,
    norm2_gain,
    weight_gate,
    weight_up,
    weight_down,
):
    logdecay = -gate_code.astype(jnp.float32) * gate_unit
    beta_rate = beta_code.astype(jnp.float32) * beta_unit
    everything = (
        norm1_gain,
        weight_in,
        conv_weight,
        out_gain,
        weight_out,
        norm2_gain,
        weight_gate,
        weight_up,
        weight_down,
    )
    stream = tokens.astype(jnp.float32)
    kept_layers = []
    for layer_idx in range(STACK_LEVELS):
        weights = tuple((tensor[layer_idx] for tensor in everything))
        stream, stored = layer_forward(stream, logdecay[layer_idx], beta_rate[layer_idx], weights)
        kept_layers.append((weights, stored))
    activations = stream.astype(jnp.bfloat16)
    grad_stream = cotangent.astype(jnp.float32)
    large_grads = []
    small_grads = []
    for layer_idx in reversed(range(STACK_LEVELS)):
        weights, stored = kept_layers[layer_idx]
        grad_stream, layer_part = layer_backward(
            grad_stream, logdecay[layer_idx], beta_rate[layer_idx], weights, stored
        )
        large_part = (layer_part[1], layer_part[4], layer_part[6], layer_part[7], layer_part[8])
        large_grads.insert(0, large_part)
        small_grads.insert(0, (layer_part[2], layer_part[0], layer_part[3], layer_part[5]))
    large_stack = tuple(
        (
            jnp.stack([grad_group[slot_index] for grad_group in large_grads])
            for slot_index in range(5)
        )
    )
    large_stack = (
        lax.psum_scatter(large_stack[0], "seq", scatter_dimension=1, tiled=True),
        lax.psum_scatter(large_stack[1], "seq", scatter_dimension=2, tiled=True),
        lax.psum_scatter(large_stack[2], "seq", scatter_dimension=1, tiled=True),
        lax.psum_scatter(large_stack[3], "seq", scatter_dimension=1, tiled=True),
        lax.psum_scatter(large_stack[4], "seq", scatter_dimension=2, tiled=True),
    )
    small_stack = tuple(
        (
            jnp.stack([grad_group[slot_index] for grad_group in small_grads])
            for slot_index in range(4)
        )
    )
    conv_grad, gain_one_grad, out_gain_grad, gain_two_grad = lax.psum(
        (small_stack[0], small_stack[1], small_stack[2], small_stack[3]), "seq"
    )
    return (
        activations,
        grad_stream,
        gain_one_grad,
        large_stack[0],
        conv_grad,
        out_gain_grad,
        large_stack[1],
        gain_two_grad,
        large_stack[2],
        large_stack[3],
        large_stack[4],
    )


def solution(mesh):
    in_specs = (
        P("seq", None),
        P("seq", None),
        P(None, "seq", "head"),
        P(None, "seq", "head"),
        P(),
        P(None, None, "head"),
        P(None, None, "head"),
        P(),
        P(None, "head", None),
        P(),
        P(None, None, "head"),
        P(None, None, "head"),
        P(None, "head", None),
    )
    out_specs = (
        P("seq", None),
        P("seq", None),
        P(),
        P(None, "seq", "head"),
        P(None, None, "head"),
        P(),
        P(None, "head", "seq"),
        P(),
        P(None, "seq", "head"),
        P(None, "seq", "head"),
        P(None, "head", "seq"),
    )
    return jax.shard_map(body, mesh=mesh, in_specs=in_specs, out_specs=out_specs, check_vma=False)
```

profile of v0, /device:TPU:0, one launch (start us, length us, event | category | flops | bytes accessed | tf_op | source)
XLA Modules:
  0.0 1594.9 jit_solution(10691709195272504350)
XLA Ops:
  9.1 5.8 slice_bitcast_fusion.4
  15.0 3.2 copy.510
  20.6 4.9 collective-permute-start
  26.3 10.4 collective-permute-done
  41.2 28.4 %while.210 = (s32[]{:T(128)}, f32[2,384,128]{2,1,0:T(8,128)S(1)}, f32[2,64,2,384]{3,1,0,2:T(8,128)S(1)}, f32[2,64,2]{1,2,0:T(2,128)S(1)}, f32[2,64,2]{1,2,0:T(2,...) while((s32[]{:T(128)}, f32[2,384,128]{2,1,0:T(8,128)S(1)}, ...), condition=%wide.region_5.7_spmd, body=%wide.region_3.6_spmd.sunk | while | flops 340353152 | bytes 4627117 | solution.py:101
  42.1 9.8 custom-call.34
  56.3 9.8 custom-call.34
  71.3 41.7 %all-gather.7.cloned.1.call-done = f32[16,128,128]{2,1,0:T(8,128)} async-done(((f32[2,128,128]{2,1,0:T(8,128)}), f32[16,128,128]{2,1,0:T(8,128)}) %all-gather.7.cloned.1.call-update) | async-done | bytes 1048592 | tf_op jit(solution)/shard_map/all_gather | solution.py:117
  113.0 50.5 %all-gather.9.cloned.1.call-done = f32[16,256,128]{2,1,0:T(8,128)} async-done(((f32[2,256,128]{2,1,0:T(8,128)}), f32[16,256,128]{2,1,0:T(8,128)}) %all-gather.9.cloned.1.call-update) | async-done | bytes 2097168 | tf_op jit(solution)/shard_map/all_gather | solution.py:118
  163.5 20.1 %while.216 = (s32[]{:T(128)}, f32[2,256,128]{1,2,0:T(8,128)S(1)}, s32[]{:T(128)}, f32[8,2,128,128]{3,2,1,0:T(8,128)}, f32[8,2,256,128]{3,2,1,0:T(8,128)}, /*index=5*/s32[]{:T(128)}, s32[]{:T(128)}) while((s32[]{:T(128)}, f32[2,256,128]{1,2,0:T(8,128)S(1)}, s32[]{:T(128)}, f32[8,2,128,128]{3,2,1,0:T(8,128)}, ...), condition=%wide.region_7.9_spmd.clone, body=%wide.region_6.8_spmd.clone.sunk | while | flops 100925440 | bytes 2754667 | solution.py:132
  187.0 20.2 %reduce-scatter.10.cloned.1.call-done = f32[128,256]{1,0:T(8,128)} async-done(((f32[128,1024]{1,0:T(8,128)}), f32[128,256]{1,0:T(8,128)}) %reduce-scatter.10.cloned.1.call-update) | async-done | bytes 131088 | tf_op jit(solution)/shard_map/reduce_scatter | solution.py:155
  207.2 6.9 all_gather.32
  219.1 4.8 copy.527
  223.9 17.5 %reduce-scatter.12.cloned.1.call-done = f32[128,256]{1,0:T(8,128)} async-done(((f32[128,1024]{1,0:T(8,128)}), f32[128,256]{1,0:T(8,128)}) %reduce-scatter.12.cloned.1.call-update) | async-done | bytes 131088 | tf_op jit(solution)/shard_map/reduce_scatter | solution.py:155
  241.4 7.0 all_gather.33
  249.2 3.1 fusion.422
  254.3 4.2 collective-permute-start.1
  259.9 9.7 collective-permute-done.1
  269.6 3.5 fusion.404
  275.9 30.3 %while.211 = (s32[]{:T(128)}, f32[2,384,128]{2,1,0:T(8,128)S(1)}, f32[2,64,2,384]{3,1,0,2:T(8,128)S(1)}, f32[2,64,2]{1,2,0:T(2,128)S(1)}, f32[2,64,2]{1,2,0:T(2,...) while((s32[]{:T(128)}, f32[2,384,128]{2,1,0:T(8,128)S(1)}, ...), condition=%wide.region_17.19_spmd, body=%wide.region_15.18_spmd.sunk | while | flops 340353152 | bytes 4627117 | solution.py:101
  276.9 9.8 custom-call.35
  292.0 9.8 custom-call.35
  307.8 41.1 %all-gather.11.cloned.1.call-done = f32[16,128,128]{2,1,0:T(8,128)} async-done(((f32[2,128,128]{2,1,0:T(8,128)}), f32[16,128,128]{2,1,0:T(8,128)}) %all-gather.11.cloned.1.call-update) | async-done | bytes 1048592 | tf_op jit(solution)/shard_map/all_gather | solution.py:117
  348.9 50.4 %all-gather.13.cloned.1.call-done = f32[16,256,128]{2,1,0:T(8,128)} async-done(((f32[2,256,128]{2,1,0:T(8,128)}), f32[16,256,128]{2,1,0:T(8,128)}) %all-gather.13.cloned.1.call-update) | async-done | bytes 2097168 | tf_op jit(solution)/shard_map/all_gather | solution.py:118
  399.3 20.0 %while.217 = (s32[]{:T(128)}, f32[2,256,128]{1,2,0:T(8,128)S(1)}, s32[]{:T(128)}, f32[8,2,128,128]{3,2,1,0:T(8,128)}, f32[8,2,256,128]{3,2,1,0:T(8,128)}, /*index=5*/s32[]{:T(128)}, s32[]{:T(128)}) while((s32[]{:T(128)}, f32[2,256,128]{1,2,0:T(8,128)S(1)}, s32[]{:T(128)}, f32[8,2,128,128]{3,2,1,0:T(8,128)}, ...), condition=%wide.region_19.21_spmd.clone, body=%wide.region_18.20_spmd.clone.sunk | while | flops 100925440 | bytes 2754667 | solution.py:132
  426.3 17.6 %reduce-scatter.14.cloned.1.call-done = f32[128,256]{1,0:T(8,128)} async-done(((f32[128,1024]{1,0:T(8,128)}), f32[128,256]{1,0:T(8,128)}) %reduce-scatter.14.cloned.1.call-update) | async-done | bytes 131088 | tf_op jit(solution)/shard_map/reduce_scatter | solution.py:155
  443.9 6.9 all_gather.36
  462.5 28.1 %all-reduce.38.cloned.1.call-done = f32[128,1024]{1,0:T(8,128)} async-done(((f32[128,1024]{1,0:T(8,128)}), f32[128,1024]{1,0:T(8,128)}) %all-reduce.38.cloned.1.call-update) | async-done | bytes 524304 | tf_op jit(solution)/shard_map/psum | solution.py:278
  492.4 23.1 %reduce-scatter.16.cloned.1.call-done = f32[128,256]{1,0:T(8,128)} async-done(((f32[128,1024]{1,0:T(8,128)}), f32[128,256]{1,0:T(8,128)}) %reduce-scatter.16.cloned.1.call-update) | async-done | bytes 131088 | tf_op jit(solution)/shard_map/reduce_scatter | solution.py:155
  515.4 7.0 all_gather.37
  535.7 39.1 %while.214 = (s32[]{:T(128)}, f32[2,256,128]{2,1,0:T(8,128)S(1)}, f32[2,2,64,64]{3,2,1,0:T(8,128)}, f32[2,64,2,1]{1,2,3,0:T(2,128)S(1)}, f32[2,64,2,1]{1,2,3,0:T...) while((s32[]{:T(128)}, f32[2,256,128]{2,1,0:T(8,128)S(1)}, ...), condition=%wide.region_31.34_spmd.clone.clone, body=%wide.region_29.33_spmd.clone.clone.sunk | while | flops 164024704 | bytes 3933053 | solution.py:101
  541.2 9.9 custom-call.38
  560.8 9.8 custom-call.38
  574.8 5.1 all-gather.15.cloned.1.call-done
  579.9 32.3 %while.218 = (s32[]{:T(128)}, f32[2,256,128]{1,2,0:T(8,128)}, s32[]{:T(128)}, f32[8,2,128,128]{3,2,1,0:T(8,128)}, f32[8,2,256,128]{3,2,1,0:T(8,128)}, /*index=5*/s32[]{:T(128)}, s32[]{:T(128)}, s32[]{:T(128)}, s32[]{:T(128)}) while((s32[]{:T(128)}, f32[2,256,128]{1,2,0:T(8,128)}, s32[]{:T(128)}, f32[8,2,128,128]{3,2,1,0:T(8,128)}, ...), condition=%wide.region_28.30_spmd.clone, body=%wide.region_27.29_spmd.clone.sunk | while | flops 100925448 | bytes 2754729 | solution.py:150
  615.2 43.8 %while.212 = (s32[]{:T(128)}, f32[2,256,128]{2,1,0:T(8,128)S(1)}, f32[2,64,2,128]{3,1,0,2:T(8,128)}, f32[2,64,2,128]{3,1,0,2:T(8,128)}, f32[2,64,2,256]{3,1,0,2:...) while((s32[]{:T(128)}, f32[2,256,128]{2,1,0:T(8,128)S(1)}, ...), condition=%wide.region_33.38_spmd.clone, body=%wide.region_32.37_spmd.clone.sunk | while | flops 485101568 | bytes 11272125 | solution.py:101
  616.1 9.8 custom-call.36
  638.0 9.8 custom-call.36
  665.4 3.6 multiply_reduce_fusion.5
  673.0 12.7 collective-permute-done.2
  686.9 3.9 fusion.332
  690.9 33.6 %all-reduce.40.cloned.1.call-done = f32[128,1024]{1,0:T(8,128)} async-done(((f32[128,1024]{1,0:T(8,128)}), f32[128,1024]{1,0:T(8,128)}) %all-reduce.40.cloned.1.call-update) | async-done | bytes 524304 | tf_op jit(solution)/shard_map/psum | solution.py:310
  731.5 33.5 %all-reduce.42.cloned.1.call-done = f32[128,1024]{1,0:T(8,128)} async-done(((f32[128,1024]{1,0:T(8,128)}), f32[128,1024]{1,0:T(8,128)}) %all-reduce.42.cloned.1.call-update) | async-done | bytes 524304 | tf_op jit(solution)/shard_map/psum | solution.py:278
  775.5 33.5 %while.215 = (s32[]{:T(128)}, f32[2,256,128]{2,1,0:T(8,128)S(1)}, f32[2,2,64,64]{3,2,1,0:T(8,128)S(1)}, f32[2,64,2,1]{1,2,3,0:T(2,128)S(1)}, f32[2,64,2,1]{1,2,3...) while((s32[]{:T(128)}, f32[2,256,128]{2,1,0:T(8,128)S(1)}, ...), condition=%wide.region_45.50_spmd.clone.clone, body=%wide.region_43.49_spmd.clone.clone.sunk | while | flops 164024704 | bytes 3990809 | solution.py:101
  780.1 9.9 custom-call.39
  796.9 9.8 custom-call.39
  809.0 14.1 all-gather.17.cloned.1.call-done
  823.1 19.6 %while.219 = (s32[]{:T(128)}, f32[2,256,128]{1,2,0:T(8,128)S(1)}, s32[]{:T(128)}, f32[8,2,128,128]{3,2,1,0:T(8,128)}, f32[8,2,256,128]{3,2,1,0:T(8,128)}, /*index=5*/s32[]{:T(128)}, s32[]{:T(128)}, s32[]{:T(128)}, s32[]{:T(128)}) while((s32[]{:T(128)}, f32[2,256,128]{1,2,0:T(8,128)S(1)}, s32[]{:T(128)}, ...), condition=%wide.region_42.47_spmd.clone, body=%wide.region_41.46_spmd.clone.sunk | while | flops 100925448 | bytes 2754729 | solution.py:150
  843.7 35.4 %while.213 = (s32[]{:T(128)}, f32[2,256,128]{2,1,0:T(8,128)S(1)}, f32[2,64,2,128]{3,1,0,2:T(8,128)S(1)}, f32[2,64,2,128]{3,1,0,2:T(8,128)S(1)}, f32[2,64,2,256]{...) while((s32[]{:T(128)}, f32[2,256,128]{2,1,0:T(8,128)S(1)}, ...), condition=%wide.region_47.52_spmd.clone, body=%wide.region_46.51_spmd.clone.sunk | while | flops 485101568 | bytes 8618345 | solution.py:101
  844.6 9.8 custom-call.37
  862.3 9.8 custom-call.37
  886.8 11.9 collective-permute-done.3
  900.9 3.9 fusion.334
  914.7 3.0 pad_maximum_fusion.1
  919.7 3.1 pad_maximum_fusion.2
  925.8 3.7 convolution_bitcast_fusion.19
  929.5 8.6 pad_maximum_fusion
  938.9 5.7 all-reduce.32
  945.9 38.6 %all-reduce.31 = (f32[2,1024]{1,0:T(2,128)}, f32[2,4,1024]{2,1,0:T(4,128)}, f32[2,256]{1,0:T(2,128)}, f32[2,1024]{1,0:T(2,128)}) all-reduce(f32[2,1024]{1,0:T(2,128)S(1)} %pad_maximum_fusion.8, f32[2,4,1024]{2,1,0:T(4,128)S(1)} %pad_maximum_fusion.7, ...), channel_id=1, replica_groups=mesh['seq'=8,'head'=4] {'seq'}, use_global_device_ids=true, to_apply=%region_54.59 | all-reduce | flops 12800 | bytes 102400 | tf_op jit(solution)/shard_map/psum | solution.py:394
  986.5 46.7 %reduce-scatter.20.cloned.1.call-done = f32[2,512,128]{2,1,0:T(8,128)} async-done(((f32[2,512,1024]{2,1,0:T(8,128)}), f32[2,512,128]{2,1,0:T(8,128)}) %reduce-scatter.20.cloned.1.call-update) | async-done | bytes 524304 | tf_op jit(solution)/shard_map/reduce_scatter | solution.py:383
  1033.2 114.8 %reduce-scatter.26.cloned.1.call-done = f32[2,704,128]{2,1,0:T(8,128)} async-done(((f32[2,704,1024]{2,1,0:T(8,128)}), f32[2,704,128]{2,1,0:T(8,128)}) %reduce-scatter.26.cloned.1.call-update) | async-done | bytes 720912 | tf_op jit(solution)/shard_map/reduce_scatter | solution.py:386
  1148.0 114.5 %reduce-scatter.22.cloned.1.call-done = f32[2,128,704]{1,2,0:T(8,128)} async-done(((f32[2,1024,704]{1,2,0:T(8,128)}), f32[2,128,704]{1,2,0:T(8,128)}) %reduce-scatter.22.cloned.1.call-update) | async-done | bytes 720912 | tf_op jit(solution)/shard_map/reduce_scatter | solution.py:384
  1262.5 114.5 %reduce-scatter.24.cloned.1.call-done = f32[2,128,704]{1,2,0:T(8,128)} async-done(((f32[2,1024,704]{1,2,0:T(8,128)}), f32[2,128,704]{1,2,0:T(8,128)}) %reduce-scatter.24.cloned.1.call-update) | async-done | bytes 720912 | tf_op jit(solution)/shard_map/reduce_scatter | solution.py:385
  1377.0 211.0 %reduce-scatter.18.cloned.1.call-done = f32[2,128,1536]{2,1,0:T(8,128)} async-done(((f32[2,1024,1536]{2,1,0:T(8,128)}), f32[2,128,1536]{2,1,0:T(8,128)}) %reduce-scatter.18.cloned.1.call-update) | async-done | bytes 1572880 | tf_op jit(solution)/shard_map/reduce_scatter | solution.py:382
  (1039 shorter events, 302.8 us)
Async XLA Ops:
  7.2 105.8 %all-gather.7.cloned.1.call-start = ((), (), s32[]{:S(2)}) async-start(), calls=%async_computation.9 | async-start | bytes 1179648 | tf_op jit(solution)/shard_map/all_gather | solution.py:117
  9.1 239.5 %copy-start.80 = (f32[1,1024]{1,0:T(1,128)}, f32[1,1024]{1,0:T(1,128)S(1)}, u32[]{:S(2)}) copy-start(f32[1,1024]{1,0:T(1,128)S(1)} %get-tuple-element.3506) | copy-start | bytes 12292
  20.6 16.1 %collective-permute-start = (f32[3,1024]{0,1:T(8,128)S(1)}, f32[3,1024]{0,1:T(8,128)S(1)}, u32[]{:S(2)}, u32[]{:S(2)}) collective-permute-start(f32[3,1024]{0,1:T(8,128)S(1)} %copy.512), channel_id=1, source_target_pairs={{0,4},{4,8},{8,12},{12,16},{16,20},{20,24},{24,28},{1,5},{5,9},{9,... | collective-permute-start | bytes 36872 | tf_op jit(solution)/shard_map/ppermute | solution.py:20
  25.7 243.9 %copy-start.102 = (f32[1,1,1024]{2,1,0:T(1,128)}, f32[1,1,1024]{2,1,0:T(1,128)S(1)}, u32[]{:S(2)}) copy-start(f32[1,1,1024]{2,1,0:T(1,128)S(1)} %get-tuple-element.3494) | copy-start | bytes 12292
  25.7 243.9 %copy-start.104 = (f32[1,1,1024]{2,1,0:T(1,128)}, f32[1,1,1024]{2,1,0:T(1,128)S(1)}, u32[]{:S(2)}) copy-start(f32[1,1,1024]{2,1,0:T(1,128)S(1)} %get-tuple-element.3495) | copy-start | bytes 12292
  25.7 243.9 %copy-start.106 = (f32[1,1,1024]{2,1,0:T(1,128)}, f32[1,1,1024]{2,1,0:T(1,128)S(1)}, u32[]{:S(2)}) copy-start(f32[1,1,1024]{2,1,0:T(1,128)S(1)} %get-tuple-element.3496) | copy-start | bytes 12292
  25.8 243.9 %copy-start.108 = (f32[1,1,1024]{2,1,0:T(1,128)}, f32[1,1,1024]{2,1,0:T(1,128)S(1)}, u32[]{:S(2)}) copy-start(f32[1,1,1024]{2,1,0:T(1,128)S(1)} %get-tuple-element.3497) | copy-start | bytes 12292
  40.8 30.4 %copy-start.155 = (f32[2,256]{1,0:T(2,128)S(1)}, f32[2,256]{1,0:T(2,128)}, u32[]{:S(2)}) copy-start(f32[2,256]{1,0:T(2,128)} %param.48) | copy-start | bytes 6148
  69.6 94.0 %copy-start.83 = (f32[2,64,2]{1,2,0:T(2,128)}, f32[2,64,2]{1,2,0:T(2,128)S(1)}, u32[]{:S(2)}) copy-start(f32[2,64,2]{1,2,0:T(2,128)S(1)} %get-tuple-element.4970) | copy-start | bytes 3076
  69.6 93.9 %copy-start.87 = (f32[2,64,2]{1,2,0:T(2,128)}, f32[2,64,2]{1,2,0:T(2,128)S(1)}, u32[]{:S(2)}) copy-start(f32[2,64,2]{1,2,0:T(2,128)S(1)} %get-tuple-element.4976) | copy-start | bytes 3076
  69.6 114.1 %copy-start.57 = (f32[2,64,2,384]{3,1,0,2:T(8,128)}, f32[2,64,2,384]{3,1,0,2:T(8,128)S(1)}, u32[]{:S(2)}) copy-start(f32[2,64,2,384]{3,1,0,2:T(8,128)S(1)} %get-tuple-element.2055) | copy-start | bytes 1179652
  70.4 93.2 %all-gather.9.cloned.1.call-start = ((), (), s32[]{:S(2)}) async-start(), calls=%async_computation.10 | async-start | bytes 2359296 | tf_op jit(solution)/shard_map/all_gather | solution.py:118
  71.1 136.0 %reduce-scatter.10.cloned.1.call-start = ((), (), s32[]{:S(2)}) async-start(), calls=%async_computation.11 | async-start | bytes 655360 | tf_op jit(solution)/shard_map/reduce_scatter | solution.py:155
  71.2 112.9 %copy-start.120 = (f32[1,256]{1,0:T(1,128)}, f32[1,256]{1,0:T(1,128)S(1)}, u32[]{:S(2)}) copy-start(f32[1,256]{1,0:T(1,128)S(1)} %get-tuple-element.3509) | copy-start | bytes 3076
  71.2 348.6 %copy-start.122 = (f32[1,256]{1,0:T(1,128)}, f32[1,256]{1,0:T(1,128)S(1)}, u32[]{:S(2)}) copy-start(f32[1,256]{1,0:T(1,128)S(1)} %get-tuple-element.3508) | copy-start | bytes 3076
  183.6 30.5 %copy-start.2 = (bf16[128,1024]{1,0:T(8,128)(2,1)S(1)}, bf16[128,1024]{1,0:T(8,128)(2,1)}, u32[]{:S(2)}) copy-start(bf16[128,1024]{1,0:T(8,128)(2,1)} %param.41) | copy-start | bytes 786436
  184.1 30.3 %copy-start.25 = (f32[128,2,256]{2,0,1:T(8,128)}, f32[128,2,256]{2,0,1:T(8,128)S(1)}, u32[]{:S(2)}) copy-start(f32[128,2,256]{2,0,1:T(8,128)S(1)} %get-tuple-element.3519) | copy-start | bytes 786436
  184.1 30.3 %copy-start.143 = (f32[128,2]{0,1:T(2,128)}, f32[128,2]{0,1:T(2,128)S(1)}, u32[]{:S(2)}) copy-start(f32[128,2]{0,1:T(2,128)S(1)} %get-tuple-element.3518) | copy-start | bytes 3076
  186.9 54.5 %reduce-scatter.12.cloned.1.call-start = ((), (), s32[]{:S(2)}) async-start(), calls=%async_computation.12 | async-start | bytes 655360 | tf_op jit(solution)/shard_map/reduce_scatter | solution.py:155
  187.0 30.9 %copy-start.90 = (f32[1,1024]{1,0:T(1,128)}, f32[1,1024]{1,0:T(1,128)S(1)}, u32[]{:S(2)}) copy-start(f32[1,1024]{1,0:T(1,128)S(1)} %get-tuple-element.3505) | copy-start | bytes 12292
  187.0 264.0 %copy-start.92 = (f32[1,1024]{1,0:T(1,128)}, f32[1,1024]{1,0:T(1,128)S(1)}, u32[]{:S(2)}) copy-start(f32[1,1024]{1,0:T(1,128)S(1)} %get-tuple-element.3504) | copy-start | bytes 12292
  219.1 129.8 %all-gather.11.cloned.1.call-start = ((), (), s32[]{:S(2)}) async-start(), calls=%async_computation.13 | async-start | bytes 1179648 | tf_op jit(solution)/shard_map/all_gather | solution.py:117
  248.6 477.8 %copy-start = (f32[128,1024]{1,0:T(8,128)}, f32[128,1024]{1,0:T(8,128)S(1)}, u32[]{:S(2)}) copy-start(f32[128,1024]{1,0:T(8,128)S(1)} %get-tuple-element.3414) | copy-start | bytes 1572868
  254.3 15.4 collective-permute-start.1
  306.2 113.2 %copy-start.58 = (f32[2,64,2,384]{3,1,0,2:T(8,128)}, f32[2,64,2,384]{3,1,0,2:T(8,128)S(1)}, u32[]{:S(2)}) copy-start(f32[2,64,2,384]{3,1,0,2:T(8,128)S(1)} %get-tuple-element.2058) | copy-start | bytes 1179652
  306.9 92.4 %all-gather.13.cloned.1.call-start = ((), (), s32[]{:S(2)}) async-start(), calls=%async_computation.14 | async-start | bytes 2359296 | tf_op jit(solution)/shard_map/all_gather | solution.py:118
  307.7 136.2 %reduce-scatter.14.cloned.1.call-start = ((), (), s32[]{:S(2)}) async-start(), calls=%async_computation.15 | async-start | bytes 655360 | tf_op jit(solution)/shard_map/reduce_scatter | solution.py:155
  419.8 105.8 %copy-start.27 = (f32[128,2,256]{2,0,1:T(8,128)}, f32[128,2,256]{2,0,1:T(8,128)S(1)}, u32[]{:S(2)}) copy-start(f32[128,2,256]{2,0,1:T(8,128)S(1)} %get-tuple-element.3523) | copy-start | bytes 786436
  423.6 67.0 %all-reduce.38.cloned.1.call-start = ((), (), s32[]{:S(2)}) async-start(), calls=%async_computation.17 | async-start | bytes 1048576 | tf_op jit(solution)/shard_map/psum | solution.py:278
  456.5 58.9 %reduce-scatter.16.cloned.1.call-start = ((), (), s32[]{:S(2)}) async-start(), calls=%async_computation.16 | async-start | bytes 655360 | tf_op jit(solution)/shard_map/reduce_scatter | solution.py:155
  459.2 31.4 %copy-start.93 = (f32[1,1024]{1,0:T(1,128)S(1)}, f32[1,1024]{1,0:T(1,128)}, u32[]{:S(2)}) copy-start(f32[1,1024]{1,0:T(1,128)} %copy-done.92) | copy-start | bytes 12292
  459.2 120.6 %all-gather.15.cloned.1.call-start = ((), (), s32[]{:S(2)}) async-start(), calls=%async_computation.18 | async-start | bytes 2359296 | tf_op jit(solution)/shard_map/all_gather | solution.py:137
  462.4 62.0 %copy-start.123 = (f32[1,256]{1,0:T(1,128)S(1)}, f32[1,256]{1,0:T(1,128)}, u32[]{:S(2)}) copy-start(f32[1,256]{1,0:T(1,128)} %copy-done.122) | copy-start | bytes 3076
  529.6 194.8 %all-reduce.40.cloned.1.call-start = ((), (), s32[]{:S(2)}) async-start(), calls=%async_computation.19 | async-start | bytes 1048576 | tf_op jit(solution)/shard_map/psum | solution.py:310
  671.4 14.3 collective-permute-start.2
  686.1 38.4 %copy-start.81 = (f32[1,1024]{1,0:T(1,128)S(1)}, f32[1,1024]{1,0:T(1,128)}, u32[]{:S(2)}) copy-start(f32[1,1024]{1,0:T(1,128)} %copy-done.80) | copy-start | bytes 12292
  686.1 38.4 %copy-start.134 = (f32[128]{0:T(128)S(1)}, f32[128]{0:T(128)}, u32[]{:S(2)}) copy-start(f32[128]{0:T(128)} %copy-done.133) | copy-start | bytes 1540
  686.9 39.5 %copy-start.161 = (f32[128]{0:T(128)S(1)}, f32[128]{0:T(128)}, u32[]{:S(2)}) copy-start(f32[128]{0:T(128)} %copy-done.160) | copy-start | bytes 1540
  686.9 39.5 %copy-start.18 = (f32[128,1024]{1,0:T(8,128)S(1)}, f32[128,1024]{1,0:T(8,128)}, u32[]{:S(2)}) copy-start(f32[128,1024]{1,0:T(8,128)} %copy-done.17) | copy-start | bytes 1572868
  690.8 37.0 %copy-start.165 = (f32[128,704]{0,1:T(8,128)S(1)}, f32[128,704]{0,1:T(8,128)}, u32[]{:S(2)}) copy-start(f32[128,704]{0,1:T(8,128)} %copy-done.164) | copy-start | bytes 1081348
  690.8 37.0 %copy-start.167 = (f32[128,704]{0,1:T(8,128)S(1)}, f32[128,704]{0,1:T(8,128)}, u32[]{:S(2)}) copy-start(f32[128,704]{0,1:T(8,128)} %get-tuple-element.3521) | copy-start | bytes 1081348
  690.8 74.1 %all-reduce.42.cloned.1.call-start = ((), (), s32[]{:S(2)}) async-start(), calls=%async_computation.20 | async-start | bytes 1048576 | tf_op jit(solution)/shard_map/psum | solution.py:278
  728.4 36.5 %copy-start.91 = (f32[1,1024]{1,0:T(1,128)S(1)}, f32[1,1024]{1,0:T(1,128)}, u32[]{:S(2)}) copy-start(f32[1,1024]{1,0:T(1,128)} %copy-done.90) | copy-start | bytes 12292
  728.4 36.5 %copy-start.150 = (f32[128]{0:T(128)S(1)}, f32[128]{0:T(128)}, u32[]{:S(2)}) copy-start(f32[128]{0:T(128)} %copy-done.149) | copy-start | bytes 1540
  728.8 38.0 %copy-start.159 = (f32[128]{0:T(128)S(1)}, f32[128]{0:T(128)}, u32[]{:S(2)}) copy-start(f32[128]{0:T(128)} %copy-done.158) | copy-start | bytes 1540
  730.1 39.0 %copy-start.10 = (f32[128,2,768]{2,0,1:T(8,128)S(1)}, f32[128,2,768]{2,0,1:T(8,128)}, u32[]{:S(2)}) copy-start(f32[128,2,768]{2,0,1:T(8,128)} %copy-done.8) | copy-start | bytes 2359300
  730.1 39.0 %copy-start.26 = (f32[128,2,256]{2,0,1:T(8,128)S(1)}, f32[128,2,256]{2,0,1:T(8,128)}, u32[]{:S(2)}) copy-start(f32[128,2,256]{2,0,1:T(8,128)} %copy-done.25) | copy-start | bytes 786436
  730.1 39.0 %copy-start.119 = (f32[128,2]{0,1:T(2,128)S(1)}, f32[128,2]{0,1:T(2,128)}, u32[]{:S(2)}) copy-start(f32[128,2]{0,1:T(2,128)} %copy-done.118) | copy-start | bytes 3076
  730.1 39.0 %copy-start.121 = (f32[1,256]{1,0:T(1,128)S(1)}, f32[1,256]{1,0:T(1,128)}, u32[]{:S(2)}) copy-start(f32[1,256]{1,0:T(1,128)} %copy-done.120) | copy-start | bytes 3076
  731.3 91.8 %all-gather.17.cloned.1.call-start = ((), (), s32[]{:S(2)}) async-start(), calls=%async_computation.21 | async-start | bytes 2359296 | tf_op jit(solution)/shard_map/all_gather | solution.py:137
  773.3 171.3 %all-reduce.44.cloned.1.call-start = ((), (), s32[]{:S(2)}) async-start(), calls=%async_computation.22 | async-start | bytes 1048576 | tf_op jit(solution)/shard_map/psum | solution.py:310
  843.6 35.5 %copy-start.31 = (f32[128,2,128]{2,0,1:T(8,128)S(1)}, f32[128,2,128]{2,0,1:T(8,128)}, u32[]{:S(2)}) copy-start(f32[128,2,128]{2,0,1:T(8,128)} %copy-done.30) | copy-start | bytes 393220
  843.6 35.6 %copy-start.142 = (f32[128,2]{0,1:T(2,128)S(1)}, f32[128,2]{0,1:T(2,128)}, u32[]{:S(2)}) copy-start(f32[128,2]{0,1:T(2,128)} %copy-done.141) | copy-start | bytes 3076
  843.6 35.6 %copy-start.139 = (f32[128,2]{0,1:T(2,128)S(1)}, f32[128,2]{0,1:T(2,128)}, u32[]{:S(2)}) copy-start(f32[128,2]{0,1:T(2,128)} %copy-done.138) | copy-start | bytes 3076
  843.6 35.8 %copy-start.29 = (f32[128,2,128]{2,0,1:T(8,128)S(1)}, f32[128,2,128]{2,0,1:T(8,128)}, u32[]{:S(2)}) copy-start(f32[128,2,128]{2,0,1:T(8,128)} %copy-done.28) | copy-start | bytes 393220
  843.7 35.9 %copy-start.146 = (f32[128,2]{0,1:T(2,128)S(1)}, f32[128,2]{0,1:T(2,128)}, u32[]{:S(2)}) copy-start(f32[128,2]{0,1:T(2,128)} %copy-done.145) | copy-start | bytes 3076
  884.7 14.0 collective-permute-start.3
  904.8 128.5 %reduce-scatter.20.cloned.1.call-start = ((), (), s32[]{:S(2)}) async-start(), calls=%async_computation.24 | async-start | bytes 4718592 | tf_op jit(solution)/shard_map/reduce_scatter | solution.py:383
  907.6 240.4 %reduce-scatter.26.cloned.1.call-start = ((), (), s32[]{:S(2)}) async-start(), calls=%async_computation.27 | async-start | bytes 6488064 | tf_op jit(solution)/shard_map/reduce_scatter | solution.py:386
  912.7 349.8 %reduce-scatter.22.cloned.1.call-start = ((), (), s32[]{:S(2)}) async-start(), calls=%async_computation.25 | async-start | bytes 6488064 | tf_op jit(solution)/shard_map/reduce_scatter | solution.py:384
  917.8 459.2 %reduce-scatter.24.cloned.1.call-start = ((), (), s32[]{:S(2)}) async-start(), calls=%async_computation.26 | async-start | bytes 6488064 | tf_op jit(solution)/shard_map/reduce_scatter | solution.py:385
  922.8 665.1 %reduce-scatter.18.cloned.1.call-start = ((), (), s32[]{:S(2)}) async-start(), calls=%async_computation.23 | async-start | bytes 14155776 | tf_op jit(solution)/shard_map/reduce_scatter | solution.py:382
  938.2 46.3 %copy-start.157 = (f32[128]{0:T(128)S(1)}, f32[128]{0:T(128)}, u32[]{:S(2)}) copy-start(f32[128]{0:T(128)} %copy-done.156) | copy-start | bytes 1540
  938.2 46.3 %copy-start.22 = (f32[128,1024]{1,0:T(8,128)S(1)}, f32[128,1024]{1,0:T(8,128)}, u32[]{:S(2)}) copy-start(f32[128,1024]{1,0:T(8,128)} %copy-done.20) | copy-start | bytes 1572868
  (148 other events, 715.9 us)
Sparse Core Ops, SparseCore 0:
  70.5 42.4 all-gather.6
  115.7 47.7 all-gather.8
  187.0 20.1 reduce-scatter.9
  219.2 22.1 reduce-scatter.11
  307.1 41.8 all-gather.10
  351.5 47.7 all-gather.12
  423.7 20.1 reduce-scatter.13
  456.6 33.9 all-reduce.37
  493.7 21.7 reduce-scatter.15
  529.8 50.0 all-gather.14
  690.9 33.4 all-reduce.39
  731.4 33.4 all-reduce.41
  773.4 49.6 all-gather.16
  904.9 34.1 all-reduce.43
  943.2 90.0 reduce-scatter.19
  1037.3 110.6 reduce-scatter.25
  1152.1 110.3 reduce-scatter.21
  1266.6 110.3 reduce-scatter.23
  1381.2 206.7 reduce-scatter.17
where the time goes:
time: 1610 us; the launch traced here: 1590 us
  waiting for transfers between devices  1020 us (63%)
  other arithmetic  197 us (12%)
  matrix products  162 us (10%)
  local copies, waits for them, and re-layouts  107 us (7%)
  blocking collectives  72.1 us (4%)
  between operations  16.9 us (1%)
    reduce_scatter x1, waiting for transfers between devices, body(): lax.psum_scatter(large_stack[0], 'seq', scatter_dimension=1, tiled=True)  211 us
    another operation x32, other arithmetic, span_step(): lax.linalg.triangular_solve(system, right_side, left_side=True, lower=True)  122 us
    reduce_scatter x1, waiting for transfers between devices, body(): lax.psum_scatter(large_stack[4], 'seq', scatter_dimension=2, tiled=True)  115 us
    reduce_scatter x1, waiting for transfers between devices, body(): lax.psum_scatter(large_stack[3], 'seq', scatter_dimension=1, tiled=True)  115 us
    reduce_scatter x1, waiting for transfers between devices, body(): lax.psum_scatter(large_stack[2], 'seq', scatter_dimension=1, tiled=True)  114 us
    all_gather x2, waiting for transfers between devices, state_prefix(): lax.all_gather(offset, 'seq', axis=0, tiled=True)  101 us
    all_gather x2, waiting for transfers between devices, state_prefix(): lax.all_gather(transfer, 'seq', axis=0, tiled=True)  82.9 us
    reduce_scatter x4, waiting for transfers between devices, head_total(): lax.psum_scatter(partial_sum, 'head', scatter_dimension=1, tiled=True)  78.4 us
  transfers between devices with their start and end apart: 23, of which 22 were waited for; matrix products, arithmetic and copies ran while one was open for 8% of the time, Pallas kernels for 0%

commit v1 on v0

--- a/solution.py
+++ b/solution.py
@@ -12,6 +12,18 @@
 norm_eps = 1e-06
 gate_unit = 1.0 / 1048576.0
 beta_unit = 1.0 / 1024.0
+
+
+def collect(array, axis, dim):
+    ways, here, lap = (lax.axis_size(axis), lax.axis_index(axis), array.shape[dim])
+    line, have = (array, 1)
+    while have < ways:
+        line = jnp.concatenate(
+            [line, lax.ppermute(line, axis, [(d, (d - have) % ways) for d in range(ways)])],
+            axis=dim,
+        )
+        have = 2 * have
+    return jnp.roll(line, here * lap, axis=dim)
 
 
 def from_behind(array, axis, by):
@@ -114,7 +126,7 @@
 
 def state_prefix(transfer, offset):
     all_transfer, all_offset = (
-        lax.all_gather(transfer, "seq", axis=0, tiled=True),
+        collect(transfer, "seq", 0),
         lax.all_gather(offset, "seq", axis=0, tiled=True),
     )
     devices = lax.axis_size("seq")

time: 1610 us -> 1560 us (0.969)
  waiting for transfers between devices: 1020 us -> 952 us
    all_gather x2 -> x0, waiting for transfers between devices: 82.9 us -> none  [state_prefix(): lax.all_gather(transfer, 'seq', axis=0, tiled=True)]
    ppermute x0 -> x6, waiting for transfers between devices: none -> 74.6 us  [collect(): lax.ppermute(line, axis, [(d, (d - have) % ways) for d in range(ways)])]
    all_gather x2, waiting for transfers between devices: 101 us -> 35.7 us  [state_prefix(): lax.all_gather(offset, 'seq', axis=0, tiled=True)]
  transfers between devices with their start and end apart: 23 -> 27, of which waited for: 22 -> 26; matrix products, arithmetic and copies ran while one was open for 8% -> 9% of each run, Pallas kernels for 0% -> 0%
where the time goes in v1:
time: 1560 us; the launch traced here: 1540 us
  waiting for transfers between devices  952 us (61%)
  other arithmetic  203 us (13%)
  matrix products  162 us (10%)
  local copies, waits for them, and re-layouts  106 us (7%)
  blocking collectives  72.5 us (5%)
  starting transfers between devices  28.8 us (2%)
  between operations  16.7 us (1%)
    reduce_scatter x1, waiting for transfers between devices, body(): lax.psum_scatter(large_stack[0], 'seq', scatter_dimension=1, tiled=True)  211 us
    another operation x32, other arithmetic, span_step(): lax.linalg.triangular_solve(system, right_side, left_side=True, lower=True)  122 us
    reduce_scatter x1, waiting for transfers between devices, body(): lax.psum_scatter(large_stack[4], 'seq', scatter_dimension=2, tiled=True)  115 us
    reduce_scatter x1, waiting for transfers between devices, body(): lax.psum_scatter(large_stack[2], 'seq', scatter_dimension=1, tiled=True)  114 us
    reduce_scatter x1, waiting for transfers between devices, body(): lax.psum_scatter(large_stack[3], 'seq', scatter_dimension=1, tiled=True)  114 us
    reduce_scatter x4, waiting for transfers between devices, head_total(): lax.psum_scatter(partial_sum, 'head', scatter_dimension=1, tiled=True)  81.5 us
    ppermute x6, waiting for transfers between devices, collect(): lax.ppermute(line, axis, [(d, (d - have) % ways) for d in range(ways)])  74.6 us
    psum x2, waiting for transfers between devices, layer_backward(): grad_normed_two = lax.psum(ffn_partial, 'head')  61.6 us
  transfers between devices with their start and end apart: 27, of which 26 were waited for; matrix products, arithmetic and copies ran while one was open for 9% of the time, Pallas kernels for 0%

profile of v1, /device:TPU:0, one launch (start us, length us, event | category | flops | bytes accessed | tf_op | source)
XLA Modules:
  0.0 1544.3 jit_solution(12526290652302533007)
XLA Ops:
  9.1 5.8 slice_bitcast_fusion.4
  20.7 4.9 collective-permute-start
  26.3 10.4 collective-permute-done
  41.3 28.4 %while.210 = (s32[]{:T(128)}, f32[2,384,128]{2,1,0:T(8,128)S(1)}, f32[2,64,2,384]{3,1,0,2:T(8,128)S(1)}, f32[2,64,2]{1,2,0:T(2,128)S(1)}, f32[2,64,2]{1,2,0:T(2,...) while((s32[]{:T(128)}, f32[2,384,128]{2,1,0:T(8,128)S(1)}, ...), condition=%wide.region_5.7_spmd, body=%wide.region_3.6_spmd.sunk | while | flops 340353152 | bytes 4627117 | solution.py:113
  42.2 9.8 custom-call.34
  56.4 9.8 custom-call.34
  70.5 5.6 collective-permute-start.1
  81.1 11.8 collective-permute-done.2
  93.1 22.7 %collective-permute-done.3 = f32[8,128,128]{2,1,0:T(8,128)S(1)} collective-permute-done((f32[8,128,128]{2,1,0:T(8,128)S(1)}, f32[8,128,128]{2,1,0:T(8,128)S(1)}, u32[]{:S(2)}, u32[]{:S(2)}) %collective-permute-start.3) | collective-permute-done | bytes 524320 | tf_op jit(solution)/shard_map/ppermute | solution.py:22
  117.7 19.2 %all-gather.5.cloned.1.call-done = f32[16,256,128]{2,1,0:T(8,128)} async-done(((f32[2,256,128]{2,1,0:T(8,128)}), f32[16,256,128]{2,1,0:T(8,128)}) %all-gather.5.cloned.1.call-update) | async-done | bytes 2097168 | tf_op jit(solution)/shard_map/all_gather | solution.py:130
  137.0 20.1 %while.216 = (s32[]{:T(128)}, f32[2,256,128]{1,2,0:T(8,128)S(1)}, s32[]{:T(128)}, f32[8,2,128,128]{3,2,1,0:T(8,128)}, f32[8,2,256,128]{3,2,1,0:T(8,128)}, /*index=5*/s32[]{:T(128)}, s32[]{:T(128)}) while((s32[]{:T(128)}, f32[2,256,128]{1,2,0:T(8,128)S(1)}, s32[]{:T(128)}, f32[8,2,128,128]{3,2,1,0:T(8,128)}, ...), condition=%wide.region_7.10_spmd.clone, body=%wide.region_6.9_spmd.clone.sunk | while | flops 100925440 | bytes 2754667 | solution.py:144
  160.4 21.4 %reduce-scatter.10.cloned.1.call-done = f32[128,256]{1,0:T(8,128)} async-done(((f32[128,1024]{1,0:T(8,128)}), f32[128,256]{1,0:T(8,128)}) %reduce-scatter.10.cloned.1.call-update) | async-done | bytes 131088 | tf_op jit(solution)/shard_map/reduce_scatter | solution.py:167
  181.8 7.4 all_gather.25
  194.2 4.8 copy.527
  199.0 17.5 %reduce-scatter.12.cloned.1.call-done = f32[128,256]{1,0:T(8,128)} async-done(((f32[128,1024]{1,0:T(8,128)}), f32[128,256]{1,0:T(8,128)}) %reduce-scatter.12.cloned.1.call-update) | async-done | bytes 131088 | tf_op jit(solution)/shard_map/reduce_scatter | solution.py:167
  216.5 6.8 all_gather.26
  229.1 4.1 collective-permute-start.4
  234.7 9.7 collective-permute-done.4
  244.4 3.5 fusion.418
  250.7 30.3 %while.211 = (s32[]{:T(128)}, f32[2,384,128]{2,1,0:T(8,128)S(1)}, f32[2,64,2,384]{3,1,0,2:T(8,128)S(1)}, f32[2,64,2]{1,2,0:T(2,128)S(1)}, f32[2,64,2]{1,2,0:T(2,...) while((s32[]{:T(128)}, f32[2,384,128]{2,1,0:T(8,128)S(1)}, ...), condition=%wide.region_17.20_spmd, body=%wide.region_15.19_spmd.sunk | while | flops 340353152 | bytes 4627117 | solution.py:113
  251.6 9.8 custom-call.35
  266.8 9.8 custom-call.35
  281.8 5.3 collective-permute-start.5
  292.2 11.7 collective-permute-done.6
  304.7 23.3 %collective-permute-done.7 = f32[8,128,128]{2,1,0:T(8,128)} collective-permute-done((f32[8,128,128]{2,1,0:T(8,128)}, f32[8,128,128]{2,1,0:T(8,128)}, u32[]{:S(2)}, u32[]{:S(2)}) %collective-permute-start.7) | collective-permute-done | bytes 524320 | tf_op jit(solution)/shard_map/ppermute | solution.py:22
  330.9 16.5 %all-gather.7.cloned.1.call-done = f32[16,256,128]{2,1,0:T(8,128)} async-done(((f32[2,256,128]{2,1,0:T(8,128)}), f32[16,256,128]{2,1,0:T(8,128)}) %all-gather.7.cloned.1.call-update) | async-done | bytes 2097168 | tf_op jit(solution)/shard_map/all_gather | solution.py:130
  347.4 20.0 %while.217 = (s32[]{:T(128)}, f32[2,256,128]{1,2,0:T(8,128)S(1)}, s32[]{:T(128)}, f32[8,2,128,128]{3,2,1,0:T(8,128)}, f32[8,2,256,128]{3,2,1,0:T(8,128)}, /*index=5*/s32[]{:T(128)}, s32[]{:T(128)}) while((s32[]{:T(128)}, f32[2,256,128]{1,2,0:T(8,128)S(1)}, s32[]{:T(128)}, f32[8,2,128,128]{3,2,1,0:T(8,128)}, ...), condition=%wide.region_19.22_spmd.clone, body=%wide.region_18.21_spmd.clone.sunk | while | flops 100925440 | bytes 2754667 | solution.py:144
  374.4 19.4 %reduce-scatter.14.cloned.1.call-done = f32[128,256]{1,0:T(8,128)} async-done(((f32[128,1024]{1,0:T(8,128)}), f32[128,256]{1,0:T(8,128)}) %reduce-scatter.14.cloned.1.call-update) | async-done | bytes 131088 | tf_op jit(solution)/shard_map/reduce_scatter | solution.py:167
  393.9 7.1 all_gather.28
  412.5 28.1 %all-reduce.38.cloned.1.call-done = f32[128,1024]{1,0:T(8,128)} async-done(((f32[128,1024]{1,0:T(8,128)}), f32[128,1024]{1,0:T(8,128)}) %all-reduce.38.cloned.1.call-update) | async-done | bytes 524304 | tf_op jit(solution)/shard_map/psum | solution.py:290
  442.5 23.0 %reduce-scatter.16.cloned.1.call-done = f32[128,256]{1,0:T(8,128)} async-done(((f32[128,1024]{1,0:T(8,128)}), f32[128,256]{1,0:T(8,128)}) %reduce-scatter.16.cloned.1.call-update) | async-done | bytes 131088 | tf_op jit(solution)/shard_map/reduce_scatter | solution.py:167
  465.5 6.9 all_gather.29
  485.3 39.2 %while.214 = (s32[]{:T(128)}, f32[2,256,128]{2,1,0:T(8,128)S(1)}, f32[2,2,64,64]{3,2,1,0:T(8,128)}, f32[2,64,2,1]{1,2,3,0:T(2,128)S(1)}, f32[2,64,2,1]{1,2,3,0:T...) while((s32[]{:T(128)}, f32[2,256,128]{2,1,0:T(8,128)S(1)}, ...), condition=%wide.region_31.35_spmd.clone.clone, body=%wide.region_29.34_spmd.clone.clone.sunk | while | flops 164024704 | bytes 3933053 | solution.py:113
  490.8 9.8 custom-call.38
  510.4 9.8 custom-call.38
  524.5 5.4 all-gather.9.cloned.1.call-done
  529.9 32.3 %while.218 = (s32[]{:T(128)}, f32[2,256,128]{1,2,0:T(8,128)}, s32[]{:T(128)}, f32[8,2,128,128]{3,2,1,0:T(8,128)}, f32[8,2,256,128]{3,2,1,0:T(8,128)}, /*index=5*/s32[]{:T(128)}, s32[]{:T(128)}, s32[]{:T(128)}, s32[]{:T(128)}) while((s32[]{:T(128)}, f32[2,256,128]{1,2,0:T(8,128)}, s32[]{:T(128)}, f32[8,2,128,128]{3,2,1,0:T(8,128)}, ...), condition=%wide.region_28.31_spmd.clone, body=%wide.region_27.30_spmd.clone.sunk | while | flops 100925448 | bytes 2754729 | solution.py:162
  565.3 43.8 %while.212 = (s32[]{:T(128)}, f32[2,256,128]{2,1,0:T(8,128)S(1)}, f32[2,64,2,128]{3,1,0,2:T(8,128)}, f32[2,64,2,128]{3,1,0,2:T(8,128)}, f32[2,64,2,256]{3,1,0,2:...) while((s32[]{:T(128)}, f32[2,256,128]{2,1,0:T(8,128)S(1)}, ...), condition=%wide.region_33.39_spmd.clone, body=%wide.region_32.38_spmd.clone.sunk | while | flops 485101568 | bytes 11272125 | solution.py:113
  566.2 9.8 custom-call.36
  588.1 9.8 custom-call.36
  615.5 3.6 multiply_reduce_fusion.5
  623.3 12.7 collective-permute-done.8
  637.1 3.9 fusion.332
  641.1 33.3 %all-reduce.40.cloned.1.call-done = f32[128,1024]{1,0:T(8,128)} async-done(((f32[128,1024]{1,0:T(8,128)}), f32[128,1024]{1,0:T(8,128)}) %all-reduce.40.cloned.1.call-update) | async-done | bytes 524304 | tf_op jit(solution)/shard_map/psum | solution.py:322
  681.5 33.4 %all-reduce.42.cloned.1.call-done = f32[128,1024]{1,0:T(8,128)} async-done(((f32[128,1024]{1,0:T(8,128)}), f32[128,1024]{1,0:T(8,128)}) %all-reduce.42.cloned.1.call-update) | async-done | bytes 524304 | tf_op jit(solution)/shard_map/psum | solution.py:290
  725.6 33.5 %while.215 = (s32[]{:T(128)}, f32[2,256,128]{2,1,0:T(8,128)S(1)}, f32[2,2,64,64]{3,2,1,0:T(8,128)S(1)}, f32[2,64,2,1]{1,2,3,0:T(2,128)S(1)}, f32[2,64,2,1]{1,2,3...) while((s32[]{:T(128)}, f32[2,256,128]{2,1,0:T(8,128)S(1)}, ...), condition=%wide.region_45.51_spmd.clone.clone, body=%wide.region_43.50_spmd.clone.clone.sunk | while | flops 164024704 | bytes 3990809 | solution.py:113
  730.1 9.8 custom-call.39
  746.9 9.8 custom-call.39
  759.0 13.7 all-gather.11.cloned.1.call-done
  772.7 19.6 %while.219 = (s32[]{:T(128)}, f32[2,256,128]{1,2,0:T(8,128)S(1)}, s32[]{:T(128)}, f32[8,2,128,128]{3,2,1,0:T(8,128)}, f32[8,2,256,128]{3,2,1,0:T(8,128)}, /*index=5*/s32[]{:T(128)}, s32[]{:T(128)}, s32[]{:T(128)}, s32[]{:T(128)}) while((s32[]{:T(128)}, f32[2,256,128]{1,2,0:T(8,128)S(1)}, s32[]{:T(128)}, ...), condition=%wide.region_42.48_spmd.clone, body=%wide.region_41.47_spmd.clone.sunk | while | flops 100925448 | bytes 2754729 | solution.py:162
  793.3 35.4 %while.213 = (s32[]{:T(128)}, f32[2,256,128]{2,1,0:T(8,128)S(1)}, f32[2,64,2,128]{3,1,0,2:T(8,128)S(1)}, f32[2,64,2,128]{3,1,0,2:T(8,128)S(1)}, f32[2,64,2,256]{...) while((s32[]{:T(128)}, f32[2,256,128]{2,1,0:T(8,128)S(1)}, ...), condition=%wide.region_47.53_spmd.clone, body=%wide.region_46.52_spmd.clone.sunk | while | flops 485101568 | bytes 8618345 | solution.py:113
  794.3 9.8 custom-call.37
  812.0 9.8 custom-call.37
  836.4 11.9 collective-permute-done.9
  850.5 3.9 fusion.334
  875.4 3.7 convolution_bitcast_fusion.19
  879.1 8.6 pad_maximum_fusion
  888.5 5.7 all-reduce.32
  895.5 38.6 %all-reduce.31 = (f32[2,1024]{1,0:T(2,128)}, f32[2,4,1024]{2,1,0:T(4,128)}, f32[2,256]{1,0:T(2,128)}, f32[2,1024]{1,0:T(2,128)}) all-reduce(f32[2,1024]{1,0:T(2,128)S(1)} %pad_maximum_fusion.12, f32[2,4,1024]{2,1,0:T(4,128)S(1)} %pad_maximum_fusion.11, ...), channel_id=1, replica_groups=mesh['seq'=8,'head'=4] {'seq'}, use_global_device_ids=true, to_apply=%region_54.60 | all-reduce | flops 12800 | bytes 102400 | tf_op jit(solution)/shard_map/psum | solution.py:406
  936.2 46.8 %reduce-scatter.20.cloned.1.call-done = f32[2,512,128]{2,1,0:T(8,128)} async-done(((f32[2,512,1024]{2,1,0:T(8,128)}), f32[2,512,128]{2,1,0:T(8,128)}) %reduce-scatter.20.cloned.1.call-update) | async-done | bytes 524304 | tf_op jit(solution)/shard_map/reduce_scatter | solution.py:395
  983.0 114.8 %reduce-scatter.26.cloned.1.call-done = f32[2,704,128]{2,1,0:T(8,128)} async-done(((f32[2,704,1024]{2,1,0:T(8,128)}), f32[2,704,128]{2,1,0:T(8,128)}) %reduce-scatter.26.cloned.1.call-update) | async-done | bytes 720912 | tf_op jit(solution)/shard_map/reduce_scatter | solution.py:398
  1097.8 114.5 %reduce-scatter.22.cloned.1.call-done = f32[2,128,704]{1,2,0:T(8,128)} async-done(((f32[2,1024,704]{1,2,0:T(8,128)}), f32[2,128,704]{1,2,0:T(8,128)}) %reduce-scatter.22.cloned.1.call-update) | async-done | bytes 720912 | tf_op jit(solution)/shard_map/reduce_scatter | solution.py:396
  1212.3 114.5 %reduce-scatter.24.cloned.1.call-done = f32[2,128,704]{1,2,0:T(8,128)} async-done(((f32[2,1024,704]{1,2,0:T(8,128)}), f32[2,128,704]{1,2,0:T(8,128)}) %reduce-scatter.24.cloned.1.call-update) | async-done | bytes 720912 | tf_op jit(solution)/shard_map/reduce_scatter | solution.py:397
  1326.7 210.8 %reduce-scatter.18.cloned.1.call-done = f32[2,128,1536]{2,1,0:T(8,128)} async-done(((f32[2,1024,1536]{2,1,0:T(8,128)}), f32[2,128,1536]{2,1,0:T(8,128)}) %reduce-scatter.18.cloned.1.call-update) | async-done | bytes 1572880 | tf_op jit(solution)/shard_map/reduce_scatter | solution.py:394
  (1051 shorter events, 329.3 us)
Async XLA Ops:
  7.2 129.8 %all-gather.5.cloned.1.call-start = ((), (), s32[]{:S(2)}) async-start(), calls=%async_computation.9 | async-start | bytes 2359296 | tf_op jit(solution)/shard_map/all_gather | solution.py:130
  9.1 214.4 %copy-start.80 = (f32[1,1024]{1,0:T(1,128)}, f32[1,1024]{1,0:T(1,128)S(1)}, u32[]{:S(2)}) copy-start(f32[1,1024]{1,0:T(1,128)S(1)} %get-tuple-element.3507) | copy-start | bytes 12292
  20.7 16.1 %collective-permute-start = (f32[3,1024]{0,1:T(8,128)S(1)}, f32[3,1024]{0,1:T(8,128)S(1)}, u32[]{:S(2)}, u32[]{:S(2)}) collective-permute-start(f32[3,1024]{0,1:T(8,128)S(1)} %copy.512), channel_id=1, source_target_pairs={{0,4},{4,8},{8,12},{12,16},{16,20},{20,24},{24,28},{1,5},{5,9},{9,... | collective-permute-start | bytes 36872 | tf_op jit(solution)/shard_map/ppermute | solution.py:32
  25.8 218.6 %copy-start.102 = (f32[1,1,1024]{2,1,0:T(1,128)}, f32[1,1,1024]{2,1,0:T(1,128)S(1)}, u32[]{:S(2)}) copy-start(f32[1,1,1024]{2,1,0:T(1,128)S(1)} %get-tuple-element.3495) | copy-start | bytes 12292
  25.8 218.6 %copy-start.104 = (f32[1,1,1024]{2,1,0:T(1,128)}, f32[1,1,1024]{2,1,0:T(1,128)S(1)}, u32[]{:S(2)}) copy-start(f32[1,1,1024]{2,1,0:T(1,128)S(1)} %get-tuple-element.3496) | copy-start | bytes 12292
  25.8 218.6 %copy-start.106 = (f32[1,1,1024]{2,1,0:T(1,128)}, f32[1,1,1024]{2,1,0:T(1,128)S(1)}, u32[]{:S(2)}) copy-start(f32[1,1,1024]{2,1,0:T(1,128)S(1)} %get-tuple-element.3497) | copy-start | bytes 12292
  25.8 218.6 %copy-start.108 = (f32[1,1,1024]{2,1,0:T(1,128)}, f32[1,1,1024]{2,1,0:T(1,128)S(1)}, u32[]{:S(2)}) copy-start(f32[1,1,1024]{2,1,0:T(1,128)S(1)} %get-tuple-element.3498) | copy-start | bytes 12292
  40.9 52.2 %copy-start.155 = (f32[2,256]{1,0:T(2,128)S(1)}, f32[2,256]{1,0:T(2,128)}, u32[]{:S(2)}) copy-start(f32[2,256]{1,0:T(2,128)} %param.50) | copy-start | bytes 6148
  69.6 67.3 %copy-start.83 = (f32[2,64,2]{1,2,0:T(2,128)}, f32[2,64,2]{1,2,0:T(2,128)S(1)}, u32[]{:S(2)}) copy-start(f32[2,64,2]{1,2,0:T(2,128)S(1)} %get-tuple-element.4973) | copy-start | bytes 3076
  69.7 67.3 %copy-start.87 = (f32[2,64,2]{1,2,0:T(2,128)}, f32[2,64,2]{1,2,0:T(2,128)S(1)}, u32[]{:S(2)}) copy-start(f32[2,64,2]{1,2,0:T(2,128)S(1)} %get-tuple-element.4979) | copy-start | bytes 3076
  69.7 87.4 %copy-start.57 = (f32[2,64,2,384]{3,1,0,2:T(8,128)}, f32[2,64,2,384]{3,1,0,2:T(8,128)S(1)}, u32[]{:S(2)}) copy-start(f32[2,64,2,384]{3,1,0,2:T(8,128)S(1)} %get-tuple-element.2056) | copy-start | bytes 1179652
  70.5 111.4 %reduce-scatter.10.cloned.1.call-start = ((), (), s32[]{:S(2)}) async-start(), calls=%async_computation.10 | async-start | bytes 655360 | tf_op jit(solution)/shard_map/reduce_scatter | solution.py:167
  70.5 8.1 collective-permute-start.1
  78.7 14.2 collective-permute-start.2
  92.9 22.8 %collective-permute-start.3 = (f32[8,128,128]{2,1,0:T(8,128)S(1)}, f32[8,128,128]{2,1,0:T(8,128)S(1)}, u32[]{:S(2)}, u32[]{:S(2)}) collective-permute-start(f32[8,128,128]{2,1,0:T(8,128)S(1)} %pad_maximum_fusion.7), channel_id=1, source_target_pairs={{0,16},{4,20},{8,24},{12,28},{16,0},{20,4},{24,8},{28,12},{1,17},{... | collective-permute-start | bytes 1572872 | tf_op jit(solution)/shard_map/ppermute | solution.py:22
  93.1 64.5 %copy-start.120 = (f32[1,256]{1,0:T(1,128)}, f32[1,256]{1,0:T(1,128)S(1)}, u32[]{:S(2)}) copy-start(f32[1,256]{1,0:T(1,128)S(1)} %get-tuple-element.3510) | copy-start | bytes 3076
  93.1 274.9 %copy-start.122 = (f32[1,256]{1,0:T(1,128)}, f32[1,256]{1,0:T(1,128)S(1)}, u32[]{:S(2)}) copy-start(f32[1,256]{1,0:T(1,128)S(1)} %get-tuple-element.3509) | copy-start | bytes 3076
  160.3 56.2 %reduce-scatter.12.cloned.1.call-start = ((), (), s32[]{:S(2)}) async-start(), calls=%async_computation.11 | async-start | bytes 655360 | tf_op jit(solution)/shard_map/reduce_scatter | solution.py:167
  160.4 32.5 %copy-start.90 = (f32[1,1024]{1,0:T(1,128)}, f32[1,1024]{1,0:T(1,128)S(1)}, u32[]{:S(2)}) copy-start(f32[1,1024]{1,0:T(1,128)S(1)} %get-tuple-element.3506) | copy-start | bytes 12292
  160.4 240.7 %copy-start.92 = (f32[1,1024]{1,0:T(1,128)}, f32[1,1024]{1,0:T(1,128)S(1)}, u32[]{:S(2)}) copy-start(f32[1,1024]{1,0:T(1,128)S(1)} %get-tuple-element.3505) | copy-start | bytes 12292
  194.2 153.3 %all-gather.7.cloned.1.call-start = ((), (), s32[]{:S(2)}) async-start(), calls=%async_computation.12 | async-start | bytes 2359296 | tf_op jit(solution)/shard_map/all_gather | solution.py:130
  223.5 452.9 %copy-start = (f32[128,1024]{1,0:T(8,128)}, f32[128,1024]{1,0:T(8,128)S(1)}, u32[]{:S(2)}) copy-start(f32[128,1024]{1,0:T(8,128)S(1)} %get-tuple-element.3415) | copy-start | bytes 1572868
  229.1 15.3 collective-permute-start.4
  280.9 86.5 %copy-start.58 = (f32[2,64,2,384]{3,1,0,2:T(8,128)}, f32[2,64,2,384]{3,1,0,2:T(8,128)S(1)}, u32[]{:S(2)}) copy-start(f32[2,64,2,384]{3,1,0,2:T(8,128)S(1)} %get-tuple-element.2059) | copy-start | bytes 1179652
  281.7 112.1 %reduce-scatter.14.cloned.1.call-start = ((), (), s32[]{:S(2)}) async-start(), calls=%async_computation.13 | async-start | bytes 655360 | tf_op jit(solution)/shard_map/reduce_scatter | solution.py:167
  281.8 7.9 collective-permute-start.5
  289.7 14.2 collective-permute-start.6
  304.7 23.3 %collective-permute-start.7 = (f32[8,128,128]{2,1,0:T(8,128)}, f32[8,128,128]{2,1,0:T(8,128)}, u32[]{:S(2)}, u32[]{:S(2)}) collective-permute-start(f32[8,128,128]{2,1,0:T(8,128)} %pad_maximum_fusion.8), channel_id=1, source_target_pairs={{0,16},{4,20},{8,24},{12,28},{16,0},{20,4},{24,8},{28,12},{1,17},{... | collective-permute-start | bytes 1572872 | tf_op jit(solution)/shard_map/ppermute | solution.py:22
  368.0 107.7 %copy-start.27 = (f32[128,2,256]{2,0,1:T(8,128)}, f32[128,2,256]{2,0,1:T(8,128)S(1)}, u32[]{:S(2)}) copy-start(f32[128,2,256]{2,0,1:T(8,128)S(1)} %get-tuple-element.3524) | copy-start | bytes 786436
  371.7 69.0 %all-reduce.38.cloned.1.call-start = ((), (), s32[]{:S(2)}) async-start(), calls=%async_computation.15 | async-start | bytes 1048576 | tf_op jit(solution)/shard_map/psum | solution.py:290
  406.6 59.0 %reduce-scatter.16.cloned.1.call-start = ((), (), s32[]{:S(2)}) async-start(), calls=%async_computation.14 | async-start | bytes 655360 | tf_op jit(solution)/shard_map/reduce_scatter | solution.py:167
  409.3 120.6 %all-gather.9.cloned.1.call-start = ((), (), s32[]{:S(2)}) async-start(), calls=%async_computation.16 | async-start | bytes 2359296 | tf_op jit(solution)/shard_map/all_gather | solution.py:149
  412.4 62.1 %copy-start.123 = (f32[1,256]{1,0:T(1,128)S(1)}, f32[1,256]{1,0:T(1,128)}, u32[]{:S(2)}) copy-start(f32[1,256]{1,0:T(1,128)} %copy-done.122) | copy-start | bytes 3076
  479.7 194.8 %all-reduce.40.cloned.1.call-start = ((), (), s32[]{:S(2)}) async-start(), calls=%async_computation.17 | async-start | bytes 1048576 | tf_op jit(solution)/shard_map/psum | solution.py:322
  621.5 14.5 collective-permute-start.8
  636.3 38.2 %copy-start.81 = (f32[1,1024]{1,0:T(1,128)S(1)}, f32[1,1024]{1,0:T(1,128)}, u32[]{:S(2)}) copy-start(f32[1,1024]{1,0:T(1,128)} %copy-done.80) | copy-start | bytes 12292
  636.3 38.2 %copy-start.134 = (f32[128]{0:T(128)S(1)}, f32[128]{0:T(128)}, u32[]{:S(2)}) copy-start(f32[128]{0:T(128)} %copy-done.133) | copy-start | bytes 1540
  637.1 39.3 %copy-start.161 = (f32[128]{0:T(128)S(1)}, f32[128]{0:T(128)}, u32[]{:S(2)}) copy-start(f32[128]{0:T(128)} %copy-done.160) | copy-start | bytes 1540
  637.1 39.3 %copy-start.18 = (f32[128,1024]{1,0:T(8,128)S(1)}, f32[128,1024]{1,0:T(8,128)}, u32[]{:S(2)}) copy-start(f32[128,1024]{1,0:T(8,128)} %copy-done.17) | copy-start | bytes 1572868
  641.0 36.8 %copy-start.165 = (f32[128,704]{0,1:T(8,128)S(1)}, f32[128,704]{0,1:T(8,128)}, u32[]{:S(2)}) copy-start(f32[128,704]{0,1:T(8,128)} %copy-done.164) | copy-start | bytes 1081348
  641.0 36.8 %copy-start.167 = (f32[128,704]{0,1:T(8,128)S(1)}, f32[128,704]{0,1:T(8,128)}, u32[]{:S(2)}) copy-start(f32[128,704]{0,1:T(8,128)} %get-tuple-element.3522) | copy-start | bytes 1081348
  641.1 73.9 %all-reduce.42.cloned.1.call-start = ((), (), s32[]{:S(2)}) async-start(), calls=%async_computation.18 | async-start | bytes 1048576 | tf_op jit(solution)/shard_map/psum | solution.py:290
  678.5 36.5 %copy-start.91 = (f32[1,1024]{1,0:T(1,128)S(1)}, f32[1,1024]{1,0:T(1,128)}, u32[]{:S(2)}) copy-start(f32[1,1024]{1,0:T(1,128)} %copy-done.90) | copy-start | bytes 12292
  678.5 36.5 %copy-start.150 = (f32[128]{0:T(128)S(1)}, f32[128]{0:T(128)}, u32[]{:S(2)}) copy-start(f32[128]{0:T(128)} %copy-done.149) | copy-start | bytes 1540
  678.9 37.9 %copy-start.159 = (f32[128]{0:T(128)S(1)}, f32[128]{0:T(128)}, u32[]{:S(2)}) copy-start(f32[128]{0:T(128)} %copy-done.158) | copy-start | bytes 1540
  680.1 38.9 %copy-start.10 = (f32[128,2,768]{2,0,1:T(8,128)S(1)}, f32[128,2,768]{2,0,1:T(8,128)}, u32[]{:S(2)}) copy-start(f32[128,2,768]{2,0,1:T(8,128)} %copy-done.8) | copy-start | bytes 2359300
  680.1 38.9 %copy-start.26 = (f32[128,2,256]{2,0,1:T(8,128)S(1)}, f32[128,2,256]{2,0,1:T(8,128)}, u32[]{:S(2)}) copy-start(f32[128,2,256]{2,0,1:T(8,128)} %copy-done.25) | copy-start | bytes 786436
  680.1 38.9 %copy-start.119 = (f32[128,2]{0,1:T(2,128)S(1)}, f32[128,2]{0,1:T(2,128)}, u32[]{:S(2)}) copy-start(f32[128,2]{0,1:T(2,128)} %copy-done.118) | copy-start | bytes 3076
  680.1 38.9 %copy-start.121 = (f32[1,256]{1,0:T(1,128)S(1)}, f32[1,256]{1,0:T(1,128)}, u32[]{:S(2)}) copy-start(f32[1,256]{1,0:T(1,128)} %copy-done.120) | copy-start | bytes 3076
  681.3 91.4 %all-gather.11.cloned.1.call-start = ((), (), s32[]{:S(2)}) async-start(), calls=%async_computation.19 | async-start | bytes 2359296 | tf_op jit(solution)/shard_map/all_gather | solution.py:149
  723.3 171.0 %all-reduce.44.cloned.1.call-start = ((), (), s32[]{:S(2)}) async-start(), calls=%async_computation.20 | async-start | bytes 1048576 | tf_op jit(solution)/shard_map/psum | solution.py:322
  793.3 35.5 %copy-start.31 = (f32[128,2,128]{2,0,1:T(8,128)S(1)}, f32[128,2,128]{2,0,1:T(8,128)}, u32[]{:S(2)}) copy-start(f32[128,2,128]{2,0,1:T(8,128)} %copy-done.30) | copy-start | bytes 393220
  793.3 35.6 %copy-start.142 = (f32[128,2]{0,1:T(2,128)S(1)}, f32[128,2]{0,1:T(2,128)}, u32[]{:S(2)}) copy-start(f32[128,2]{0,1:T(2,128)} %copy-done.141) | copy-start | bytes 3076
  793.3 35.6 %copy-start.139 = (f32[128,2]{0,1:T(2,128)S(1)}, f32[128,2]{0,1:T(2,128)}, u32[]{:S(2)}) copy-start(f32[128,2]{0,1:T(2,128)} %copy-done.138) | copy-start | bytes 3076
  793.3 35.8 %copy-start.29 = (f32[128,2,128]{2,0,1:T(8,128)S(1)}, f32[128,2,128]{2,0,1:T(8,128)}, u32[]{:S(2)}) copy-start(f32[128,2,128]{2,0,1:T(8,128)} %copy-done.28) | copy-start | bytes 393220
  793.3 35.9 %copy-start.146 = (f32[128,2]{0,1:T(2,128)S(1)}, f32[128,2]{0,1:T(2,128)}, u32[]{:S(2)}) copy-start(f32[128,2]{0,1:T(2,128)} %copy-done.145) | copy-start | bytes 3076
  834.4 14.0 collective-permute-start.9
  854.4 128.6 %reduce-scatter.20.cloned.1.call-start = ((), (), s32[]{:S(2)}) async-start(), calls=%async_computation.22 | async-start | bytes 4718592 | tf_op jit(solution)/shard_map/reduce_scatter | solution.py:395
  857.2 240.5 %reduce-scatter.26.cloned.1.call-start = ((), (), s32[]{:S(2)}) async-start(), calls=%async_computation.25 | async-start | bytes 6488064 | tf_op jit(solution)/shard_map/reduce_scatter | solution.py:398
  862.3 350.0 %reduce-scatter.22.cloned.1.call-start = ((), (), s32[]{:S(2)}) async-start(), calls=%async_computation.23 | async-start | bytes 6488064 | tf_op jit(solution)/shard_map/reduce_scatter | solution.py:396
  867.4 459.3 %reduce-scatter.24.cloned.1.call-start = ((), (), s32[]{:S(2)}) async-start(), calls=%async_computation.24 | async-start | bytes 6488064 | tf_op jit(solution)/shard_map/reduce_scatter | solution.py:397
  872.5 665.1 %reduce-scatter.18.cloned.1.call-start = ((), (), s32[]{:S(2)}) async-start(), calls=%async_computation.21 | async-start | bytes 14155776 | tf_op jit(solution)/shard_map/reduce_scatter | solution.py:394
  887.8 46.4 %copy-start.157 = (f32[128]{0:T(128)S(1)}, f32[128]{0:T(128)}, u32[]{:S(2)}) copy-start(f32[128]{0:T(128)} %copy-done.156) | copy-start | bytes 1540
  887.8 46.4 %copy-start.22 = (f32[128,1024]{1,0:T(8,128)S(1)}, f32[128,1024]{1,0:T(8,128)}, u32[]{:S(2)}) copy-start(f32[128,1024]{1,0:T(8,128)} %copy-done.20) | copy-start | bytes 1572868
  (152 other events, 844.2 us)
Sparse Core Ops, SparseCore 0:
  70.6 66.2 all-gather.4
  160.4 21.3 reduce-scatter.9
  194.3 22.1 reduce-scatter.11
  281.9 65.5 all-gather.6
  371.8 21.9 reduce-scatter.13
  406.7 33.9 all-reduce.37
  443.7 21.7 reduce-scatter.15
  479.8 49.9 all-gather.8
  641.2 33.2 all-reduce.39
  681.4 33.4 all-reduce.41
  723.4 49.2 all-gather.10
  854.5 34.1 all-reduce.43
  892.9 90.0 reduce-scatter.19
  987.1 110.6 reduce-scatter.25
  1101.9 110.3 reduce-scatter.21
  1216.4 110.3 reduce-scatter.23
  1330.7 206.7 reduce-scatter.17
